TPU v7x, 32 devices: a whole 2x2x4 slice. The times are simulated.
32 devices in a mesh: tm: 8 (over y, x, core), space: 4 (over z).
Axes of the slice: x: 2, y: 2, z: 4, core: 2. Of those that a mesh axis runs over, the one named last changes fastest.
Arguments:
- hits: int32 [64, 128, 256], P('tm', 'space'), may hold values from 0 to 12
- misses: int32 [64, 128, 256], P('tm', 'space'), may hold values from 0 to 12
Outputs:
- occupancy: float32 [64, 128, 256], P('tm', 'space')
- spread: float32 [64, 128, 256], P('tm', 'space')
All inputs are finite; a program needn't handle non-finite values.
Results may differ from a plain program's by a relative error of at most 0.00019.
Values sent between devices are 32-bit elements; how exact they have to be, the bound alone decides.
A program may use at most 64 MiB of HBM per device.

v0:
```python
import math

import jax
import jax.numpy as jnp
from jax import lax
from jax.sharding import PartitionSpec as P

RADIUS = 7
SCALE_T = 64


sigma_cells = 3.0
prior_var = 4.0


def extended(shard, sides, width):
    for axis, dim in sides:
        peers, length = (lax.axis_size(axis), shard.shape[dim])
        up = [(i, (i + 1) % peers) for i in range(peers - 1)]
        down = [(j, i) for i, j in up]
        last = lax.slice_in_dim(shard, length - width, length, axis=dim)
        first = lax.slice_in_dim(shard, 0, width, axis=dim)
        before = lax.ppermute(last, axis, up)
        after = lax.ppermute(first, axis, down)
        shard = jnp.concatenate([before, shard, after], axis=dim)
    return shard


def from_behind(shard, axis, by):
    peers = lax.axis_size(axis)
    pairs = [(i, i + by) for i in range(peers) if 0 <= i + by < peers]
    return lax.ppermute(shard, axis, pairs)


def mat_mul(a, b):
    return (
        a[0] * b[0] + a[1] * b[2],
        a[0] * b[1] + a[1] * b[3],
        a[2] * b[0] + a[3] * b[2],
        a[2] * b[1] + a[3] * b[3],
    )


def mat_add(a, b):
    return tuple((x + y for x, y in zip(a, b)))


def mat_sub(a, b):
    return tuple((x - y for x, y in zip(a, b)))


def transpose(a):
    return (a[0], a[2], a[1], a[3])


def as_full(s):
    return (s[0], s[1], s[1], s[2])


def as_sym(a):
    return (a[0], 0.5 * (a[1] + a[2]), a[3])


def mat_vec(a, v):
    return (a[0] * v[0] + a[1] * v[1], a[2] * v[0] + a[3] * v[1])


def vec_add(u, v):
    return (u[0] + v[0], u[1] + v[1])


def vec_sub(u, v):
    return (u[0] - v[0], u[1] - v[1])


def inverse(a):
    determ = a[0] * a[3] - a[1] * a[2]
    return (a[3] / determ, -a[1] / determ, -a[2] / determ, a[0] / determ)


def dynamics():
    decay_rate = math.sqrt(3.0) / SCALE_T
    factor = math.exp(-decay_rate)
    transit = (
        factor * (1.0 + decay_rate),
        factor,
        -factor * decay_rate * decay_rate,
        factor * (1.0 - decay_rate),
    )
    prior_p = (prior_var, 0.0, prior_var * decay_rate * decay_rate)
    carried = mat_mul(mat_mul(transit, as_full(prior_p)), transpose(transit))
    noise_q = (
        prior_p[0] - carried[0],
        prior_p[1] - 0.5 * (carried[1] + carried[2]),
        prior_p[2] - carried[3],
    )
    return (transit, prior_p, noise_q)


def kernel_taps():
    offsets = jnp.arange(-RADIUS, RADIUS + 1).astype(jnp.float32)
    weights = jnp.exp(-offsets * offsets / (2.0 * sigma_cells * sigma_cells))
    return weights / jnp.sum(weights)


def band_matrix(col_count):
    offsets = jnp.arange(-RADIUS, RADIUS + 1).astype(jnp.float32)
    total = jnp.sum(jnp.exp(-offsets * offsets / (2.0 * sigma_cells * sigma_cells)))
    index = jnp.arange(col_count)
    offset = (index[:, None] - index[None, :]).astype(jnp.float32)
    weights = jnp.exp(-offset * offset / (2.0 * sigma_cells * sigma_cells)) / total
    return jnp.where(jnp.abs(offset) <= RADIUS, weights, jnp.zeros_like(weights))


def filter_element(num_val, den_val, is_first, transit, prior_p, noise_q, zeros_cell):
    scale_s = 1.0 + noise_q[0] * den_val
    inv_s = den_val / scale_s
    scaled_obs = num_val / scale_s
    gain_a = noise_q[0] * inv_s
    gain_b = noise_q[1] * inv_s
    general = (
        (1.0 - gain_a) * transit[0],
        (1.0 - gain_a) * transit[1],
        transit[2] - gain_b * transit[0],
        transit[3] - gain_b * transit[1],
        noise_q[0] * scaled_obs,
        noise_q[1] * scaled_obs,
        (1.0 - gain_a) * noise_q[0],
        (1.0 - gain_a) * noise_q[1],
        noise_q[2] - gain_b * noise_q[1],
        transit[0] * scaled_obs,
        transit[1] * scaled_obs,
        transit[0] * transit[0] * inv_s,
        transit[0] * transit[1] * inv_s,
        transit[1] * transit[1] * inv_s,
    )
    scale_first = 1.0 + prior_p[0] * den_val
    gain_first = prior_p[0] * den_val / scale_first
    first = (
        zeros_cell,
        zeros_cell,
        zeros_cell,
        zeros_cell,
        prior_p[0] * num_val / scale_first,
        zeros_cell,
        (1.0 - gain_first) * prior_p[0],
        zeros_cell,
        zeros_cell + prior_p[2],
        zeros_cell,
        zeros_cell,
        zeros_cell,
        zeros_cell,
        zeros_cell,
    )
    return tuple((jnp.where(is_first, x, y) for x, y in zip(first, general)))


def state_element(state_five, zeros_cell):
    return (zeros_cell,) * 4 + tuple((state_five[i] for i in range(5))) + (zeros_cell,) * 5


def combine_filter(earlier, later):
    trans_i, offs_i, cov_i, info_i, prec_i = (
        earlier[0:4],
        earlier[4:6],
        earlier[6:9],
        earlier[9:11],
        earlier[11:14],
    )
    trans_j, offs_j, cov_j, info_j, prec_j = (
        later[0:4],
        later[4:6],
        later[6:9],
        later[9:11],
        later[11:14],
    )
    product = mat_mul(as_full(cov_i), as_full(prec_j))
    solver = inverse((1.0 + product[0], product[1], product[2], 1.0 + product[3]))
    joined = mat_mul(trans_j, solver)
    trans_new = mat_mul(joined, trans_i)
    offs_new = vec_add(mat_vec(joined, vec_add(offs_i, mat_vec(as_full(cov_i), info_j))), offs_j)
    cov_new = as_sym(
        mat_add(mat_mul(mat_mul(joined, as_full(cov_i)), transpose(trans_j)), as_full(cov_j))
    )
    back_map = mat_mul(transpose(trans_i), transpose(solver))
    info_new = vec_add(mat_vec(back_map, vec_sub(info_j, mat_vec(as_full(prec_j), offs_i))), info_i)
    prec_new = as_sym(
        mat_add(mat_mul(mat_mul(back_map, as_full(prec_j)), trans_i), as_full(prec_i))
    )
    return trans_new + offs_new + cov_new + info_new + prec_new


def smoother_element(filt_five, is_last, transit, noise_q, zeros_cell):
    mean_two = filt_five[:2]
    cov = as_full(filt_five[2:])
    predicted = mat_add(mat_mul(mat_mul(transit, cov), transpose(transit)), as_full(noise_q))
    gain_mat = mat_mul(mat_mul(cov, transpose(transit)), inverse(predicted))
    shaped = mat_mul(gain_mat, transit)
    offset = vec_sub(mean_two, mat_vec(shaped, mean_two))
    leftover = as_sym(mat_sub(cov, mat_mul(shaped, cov)))
    general = gain_mat + offset + leftover
    final = (zeros_cell,) * 4 + tuple(mean_two) + tuple(filt_five[2:])
    return tuple((jnp.where(is_last, x, y) for x, y in zip(final, general)))


def combine_smooth(higher, lower):
    map_h, offs_h, cov_h = (higher[0:4], higher[4:6], higher[6:9])
    map_l, offs_l, cov_l = (lower[0:4], lower[4:6], lower[6:9])
    map_new = mat_mul(map_l, map_h)
    offs_new = vec_add(mat_vec(map_l, offs_h), offs_l)
    cov_new = as_sym(
        mat_add(mat_mul(mat_mul(map_l, as_full(cov_h)), transpose(map_l)), as_full(cov_l))
    )
    return map_new + offs_new + cov_new


def body(hits, misses):
    count_total = (hits + misses).astype(jnp.float32)
    hit_plus = hits.astype(jnp.float32) + 1.0
    miss_plus = misses.astype(jnp.float32) + 1.0
    both_plus = hit_plus + miss_plus
    weight = count_total * hit_plus * miss_plus / (both_plus * both_plus)
    logit = jnp.log(hit_plus / miss_plus)
    channels = jnp.stack([weight * logit, weight])
    row_count = channels.shape[2]
    col_count = channels.shape[3]
    padded = extended(channels, (("space", 2),), RADIUS)
    taps_row = kernel_taps()
    rowsum = jnp.zeros_like(channels)
    for shift_row in range(2 * RADIUS + 1):
        rowsum = rowsum + taps_row[shift_row] * padded[:, :, shift_row : shift_row + row_count, :]
    colsum = jnp.dot(
        rowsum.reshape(-1, col_count),
        band_matrix(col_count),
        precision=lax.Precision.HIGHEST,
        preferred_element_type=jnp.float32,
    ).reshape(channels.shape)
    numerator = colsum[0]
    denominator = colsum[1]
    transit, prior_p, noise_q = dynamics()
    tm_index = lax.axis_index("tm")
    tm_count = lax.axis_size("tm")
    frame_count = hits.shape[0]
    zeros_cell = jnp.zeros(numerator.shape[1:], jnp.float32)
    elements = []
    for f in range(frame_count):
        is_first = jnp.logical_and(tm_index == 0, f == 0)
        elements.append(
            filter_element(
                numerator[f], denominator[f], is_first, transit, prior_p, noise_q, zeros_cell
            )
        )
    summary = elements[0]
    for element in elements[1:]:
        summary = combine_filter(summary, element)

    def relay_filter(turn, incoming):
        merged = combine_filter(state_element(incoming, zeros_cell), summary)
        return from_behind(jnp.stack(merged[4:9]), "tm", 1)

    incoming = lax.fori_loop(
        0, tm_count - 1, relay_filter, jnp.zeros((5,) + zeros_cell.shape, jnp.float32)
    )
    prefix = state_element(incoming, zeros_cell)
    running = prefix
    filtered = []
    for element in elements:
        running = combine_filter(running, element)
        filtered.append(running[4:9])
    back_elements = []
    for f in range(frame_count):
        is_last = jnp.logical_and(tm_index == tm_count - 1, f == frame_count - 1)
        back_elements.append(smoother_element(filtered[f], is_last, transit, noise_q, zeros_cell))
    back_summary = back_elements[-1]
    for element in reversed(back_elements[:-1]):
        back_summary = combine_smooth(back_summary, element)

    def relay_smooth(turn, incoming):
        later_state = (zeros_cell,) * 4 + tuple((incoming[i] for i in range(5)))
        merged = combine_smooth(later_state, back_summary)
        return from_behind(jnp.stack(merged[4:9]), "tm", -1)

    incoming_back = lax.fori_loop(
        0, tm_count - 1, relay_smooth, jnp.zeros((5,) + zeros_cell.shape, jnp.float32)
    )
    suffix = (zeros_cell,) * 4 + tuple((incoming_back[i] for i in range(5)))
    running_back = suffix
    means = [None] * frame_count
    variances = [None] * frame_count
    for f in reversed(range(frame_count)):
        running_back = combine_smooth(running_back, back_elements[f])
        means[f] = running_back[4]
        variances[f] = running_back[6]
    occupancy = jax.nn.sigmoid(jnp.stack(means))
    spread = jnp.stack(variances)
    return (occupancy, spread)


def solution(mesh):
    placed = (P("tm", "space", None), P("tm", "space", None))
    return jax.shard_map(
        body,
        mesh=mesh,
        in_specs=placed,
        out_specs=(P("tm", "space", None), P("tm", "space", None)),
        check_vma=False,
    )
```

profile of v0, /device:TPU:3, one launch (start us, length us, event | category | flops | bytes accessed | tf_op | source)
XLA Modules:
  0.0 141.9 jit_solution(5157757073002425678)
XLA Ops:
  0.6 1.3 multiply_bitcast_fusion
  2.0 3.2 %collective-permute-start.2 = (f32[2,8,7,256]{3,2,1,0:T(8,128)S(1)}, f32[2,8,7,256]{3,2,1,0:T(8,128)S(1)}, u32[]{:S(2)}, u32[]{:S(2)}) collective-permute-start(f32[2,8,7,256]{3,2,1,0:T(8,128)S(1)} %get-tuple-element.470), channel_id=1, source_target_pairs={{0,1},{1,2},{2,3},{4,5},{5,6},{6,7},{8,9},{9,10},{10,11},{12,13},{... | collective-permute-start | bytes 344072 | tf_op jit(solution)/shard_map/ppermute | solution.py:23
  5.2 1.3 collective-permute-start.3
  6.5 0.6 fusion.125
  7.1 0.7 broadcast_divide_fusion
  7.8 0.7 fusion.164
  8.5 2.4 %collective-permute-done.3 = f32[2,8,7,256]{3,2,1,0:T(8,128)S(1)} collective-permute-done((f32[2,8,7,256]{3,2,1,0:T(8,128)S(1)}, f32[2,8,7,256]{3,2,1,0:T(8,128)S(1)}, u32[]{:S(2)}, u32[]{:S(2)}) %collective-permute-start.3) | collective-permute-done | bytes 114720 | tf_op jit(solution)/shard_map/ppermute | solution.py:24
  11.1 10.3 %fusion.50 = f32[2,8,32,256]{3,2,1,0:T(8,128)S(1)} fusion(f32[1,8,32,256]{3,2,1,0:T(8,128)S(1)} %get-tuple-element.473, f32[1,8,32,256]{3,2,1,0:T(8,128)S(1)} %get-tuple-element.472, f32[2,8,39,256]{3,2,1,0:T(8,128)S(1)} %get-tuple-element.469, f32[2,8,39,256]{3,2,1,0:T(8,128)S(1)} %get-tuple-element.468, f32[]{:T(128)} %bitcast.39, f32[]{:T(128)} %bitcast.38, ...), kind=kLoop, calls=%fused_computation.124 | loop fusion | flops 3932160 | bytes 8388668 | tf_op jit(solution)/shard_map/add | solution.py:231
  21.4 1.3 fusion.61
  24.2 0.4 add_add_fusion.152
  24.5 0.6 add_add_fusion.156
  25.2 0.6 add_add_fusion.157
  26.2 0.4 add_add_fusion.183
  26.5 0.6 add_multiply_fusion.20
  27.5 54.0 %while.20 = (s32[]{:T(128)}, f32[5,32,256]{2,1,0:T(8,128)S(1)}, f32[32,256]{1,0:T(8,128)S(1)}, f32[32,256]{1,0:T(8,128)S(1)}, f32[32,256]{1,0:T(8,128)S(1)}, /*i...) while((s32[]{:T(128)}, f32[5,32,256]{2,1,0:T(8,128)S(1)}, ...), condition=%wide.region_2.3_spmd, body=%wide.region_1.0_spmd.sunk | while | flops 827393 | bytes 2785477 | solution.py:261
  27.7 5.1 %collective-permute-start = (f32[5,32,256]{2,1,0:T(8,128)S(1)}, f32[5,32,256]{2,1,0:T(8,128)S(1)}, u32[]{:S(2)}, u32[]{:S(2)}) collective-permute-start(f32[5,32,256]{2,1,0:T(8,128)S(1)} %fusion.180), channel_id=1, source_target_pairs={{0,4},{4,8},{8,12},{12,16},{16,20},{20,24},{24,28},{1,5},{5,9},{9,... | collective-permute-start | bytes 491528 | tf_op jit(solution)/shard_map/while/body/eval_jaxpr/ppermute | solution.py:32
  32.9 2.2 %collective-permute-done = f32[5,32,256]{2,1,0:T(8,128)S(1)} collective-permute-done((f32[5,32,256]{2,1,0:T(8,128)S(1)}, f32[5,32,256]{2,1,0:T(8,128)S(1)}, u32[]{:S(2)}, u32[]{:S(2)}) %collective-permute-start) | collective-permute-done | bytes 163872 | tf_op jit(solution)/shard_map/while/body/eval_jaxpr/ppermute | solution.py:32
  35.3 5.3 %collective-permute-start = (f32[5,32,256]{2,1,0:T(8,128)S(1)}, f32[5,32,256]{2,1,0:T(8,128)S(1)}, u32[]{:S(2)}, u32[]{:S(2)}) collective-permute-start(f32[5,32,256]{2,1,0:T(8,128)S(1)} %fusion.180), channel_id=1, source_target_pairs={{0,4},{4,8},{8,12},{12,16},{16,20},{20,24},{24,28},{1,5},{5,9},{9,... | collective-permute-start | bytes 491528 | tf_op jit(solution)/shard_map/while/body/eval_jaxpr/ppermute | solution.py:32
  40.6 2.2 %collective-permute-done = f32[5,32,256]{2,1,0:T(8,128)S(1)} collective-permute-done((f32[5,32,256]{2,1,0:T(8,128)S(1)}, f32[5,32,256]{2,1,0:T(8,128)S(1)}, u32[]{:S(2)}, u32[]{:S(2)}) %collective-permute-start) | collective-permute-done | bytes 163872 | tf_op jit(solution)/shard_map/while/body/eval_jaxpr/ppermute | solution.py:32
  43.0 5.3 %collective-permute-start = (f32[5,32,256]{2,1,0:T(8,128)S(1)}, f32[5,32,256]{2,1,0:T(8,128)S(1)}, u32[]{:S(2)}, u32[]{:S(2)}) collective-permute-start(f32[5,32,256]{2,1,0:T(8,128)S(1)} %fusion.180), channel_id=1, source_target_pairs={{0,4},{4,8},{8,12},{12,16},{16,20},{20,24},{24,28},{1,5},{5,9},{9,... | collective-permute-start | bytes 491528 | tf_op jit(solution)/shard_map/while/body/eval_jaxpr/ppermute | solution.py:32
  48.3 2.2 %collective-permute-done = f32[5,32,256]{2,1,0:T(8,128)S(1)} collective-permute-done((f32[5,32,256]{2,1,0:T(8,128)S(1)}, f32[5,32,256]{2,1,0:T(8,128)S(1)}, u32[]{:S(2)}, u32[]{:S(2)}) %collective-permute-start) | collective-permute-done | bytes 163872 | tf_op jit(solution)/shard_map/while/body/eval_jaxpr/ppermute | solution.py:32
  50.8 5.3 %collective-permute-start = (f32[5,32,256]{2,1,0:T(8,128)S(1)}, f32[5,32,256]{2,1,0:T(8,128)S(1)}, u32[]{:S(2)}, u32[]{:S(2)}) collective-permute-start(f32[5,32,256]{2,1,0:T(8,128)S(1)} %fusion.180), channel_id=1, source_target_pairs={{0,4},{4,8},{8,12},{12,16},{16,20},{20,24},{24,28},{1,5},{5,9},{9,... | collective-permute-start | bytes 491528 | tf_op jit(solution)/shard_map/while/body/eval_jaxpr/ppermute | solution.py:32
  56.1 2.2 %collective-permute-done = f32[5,32,256]{2,1,0:T(8,128)S(1)} collective-permute-done((f32[5,32,256]{2,1,0:T(8,128)S(1)}, f32[5,32,256]{2,1,0:T(8,128)S(1)}, u32[]{:S(2)}, u32[]{:S(2)}) %collective-permute-start) | collective-permute-done | bytes 163872 | tf_op jit(solution)/shard_map/while/body/eval_jaxpr/ppermute | solution.py:32
  58.5 5.3 %collective-permute-start = (f32[5,32,256]{2,1,0:T(8,128)S(1)}, f32[5,32,256]{2,1,0:T(8,128)S(1)}, u32[]{:S(2)}, u32[]{:S(2)}) collective-permute-start(f32[5,32,256]{2,1,0:T(8,128)S(1)} %fusion.180), channel_id=1, source_target_pairs={{0,4},{4,8},{8,12},{12,16},{16,20},{20,24},{24,28},{1,5},{5,9},{9,... | collective-permute-start | bytes 491528 | tf_op jit(solution)/shard_map/while/body/eval_jaxpr/ppermute | solution.py:32
  63.8 2.2 %collective-permute-done = f32[5,32,256]{2,1,0:T(8,128)S(1)} collective-permute-done((f32[5,32,256]{2,1,0:T(8,128)S(1)}, f32[5,32,256]{2,1,0:T(8,128)S(1)}, u32[]{:S(2)}, u32[]{:S(2)}) %collective-permute-start) | collective-permute-done | bytes 163872 | tf_op jit(solution)/shard_map/while/body/eval_jaxpr/ppermute | solution.py:32
  66.3 5.3 %collective-permute-start = (f32[5,32,256]{2,1,0:T(8,128)S(1)}, f32[5,32,256]{2,1,0:T(8,128)S(1)}, u32[]{:S(2)}, u32[]{:S(2)}) collective-permute-start(f32[5,32,256]{2,1,0:T(8,128)S(1)} %fusion.180), channel_id=1, source_target_pairs={{0,4},{4,8},{8,12},{12,16},{16,20},{20,24},{24,28},{1,5},{5,9},{9,... | collective-permute-start | bytes 491528 | tf_op jit(solution)/shard_map/while/body/eval_jaxpr/ppermute | solution.py:32
  71.6 2.2 %collective-permute-done = f32[5,32,256]{2,1,0:T(8,128)S(1)} collective-permute-done((f32[5,32,256]{2,1,0:T(8,128)S(1)}, f32[5,32,256]{2,1,0:T(8,128)S(1)}, u32[]{:S(2)}, u32[]{:S(2)}) %collective-permute-start) | collective-permute-done | bytes 163872 | tf_op jit(solution)/shard_map/while/body/eval_jaxpr/ppermute | solution.py:32
  74.0 5.3 %collective-permute-start = (f32[5,32,256]{2,1,0:T(8,128)S(1)}, f32[5,32,256]{2,1,0:T(8,128)S(1)}, u32[]{:S(2)}, u32[]{:S(2)}) collective-permute-start(f32[5,32,256]{2,1,0:T(8,128)S(1)} %fusion.180), channel_id=1, source_target_pairs={{0,4},{4,8},{8,12},{12,16},{16,20},{20,24},{24,28},{1,5},{5,9},{9,... | collective-permute-start | bytes 491528 | tf_op jit(solution)/shard_map/while/body/eval_jaxpr/ppermute | solution.py:32
  79.3 2.2 %collective-permute-done = f32[5,32,256]{2,1,0:T(8,128)S(1)} collective-permute-done((f32[5,32,256]{2,1,0:T(8,128)S(1)}, f32[5,32,256]{2,1,0:T(8,128)S(1)}, u32[]{:S(2)}, u32[]{:S(2)}) %collective-permute-start) | collective-permute-done | bytes 163872 | tf_op jit(solution)/shard_map/while/body/eval_jaxpr/ppermute | solution.py:32
  81.5 0.8 multiply_add_fusion.141
  82.4 0.7 add_add_fusion.51
  85.0 54.4 %while.21 = (s32[]{:T(128)}, f32[5,32,256]{2,1,0:T(8,128)S(1)}, f32[32,256]{1,0:T(8,128)S(1)}, f32[32,256]{1,0:T(8,128)S(1)}, f32[32,256]{1,0:T(8,128)S(1)}, /*i...) while((s32[]{:T(128)}, f32[5,32,256]{2,1,0:T(8,128)S(1)}, ...), condition=%wide.region_4.5_spmd, body=%wide.region_3.4_spmd.sunk | while | flops 409601 | bytes 1802397 | solution.py:283
  85.1 1.9 %collective-permute-start.1 = (f32[5,32,256]{2,1,0:T(8,128)S(1)}, f32[5,32,256]{2,1,0:T(8,128)S(1)}, u32[]{:S(2)}, u32[]{:S(2)}) collective-permute-start(f32[5,32,256]{2,1,0:T(8,128)S(1)} %fusion.185), channel_id=1, source_target_pairs={{4,0},{8,4},{12,8},{16,12},{20,16},{24,20},{28,24},{5,1},{9,5},{13... | collective-permute-start | bytes 491528 | tf_op jit(solution)/shard_map/while/body/eval_jaxpr/ppermute | solution.py:32
  87.1 6.4 %collective-permute-done.1 = f32[5,32,256]{2,1,0:T(8,128)S(1)} collective-permute-done((f32[5,32,256]{2,1,0:T(8,128)S(1)}, f32[5,32,256]{2,1,0:T(8,128)S(1)}, u32[]{:S(2)}, u32[]{:S(2)}) %collective-permute-start.1) | collective-permute-done | bytes 163872 | tf_op jit(solution)/shard_map/while/body/eval_jaxpr/ppermute | solution.py:32
  93.5 1.9 %collective-permute-start.1 = (f32[5,32,256]{2,1,0:T(8,128)S(1)}, f32[5,32,256]{2,1,0:T(8,128)S(1)}, u32[]{:S(2)}, u32[]{:S(2)}) collective-permute-start(f32[5,32,256]{2,1,0:T(8,128)S(1)} %fusion.185), channel_id=1, source_target_pairs={{4,0},{8,4},{12,8},{16,12},{20,16},{24,20},{28,24},{5,1},{9,5},{13... | collective-permute-start | bytes 491528 | tf_op jit(solution)/shard_map/while/body/eval_jaxpr/ppermute | solution.py:32
  95.5 5.6 %collective-permute-done.1 = f32[5,32,256]{2,1,0:T(8,128)S(1)} collective-permute-done((f32[5,32,256]{2,1,0:T(8,128)S(1)}, f32[5,32,256]{2,1,0:T(8,128)S(1)}, u32[]{:S(2)}, u32[]{:S(2)}) %collective-permute-start.1) | collective-permute-done | bytes 163872 | tf_op jit(solution)/shard_map/while/body/eval_jaxpr/ppermute | solution.py:32
  101.2 1.9 %collective-permute-start.1 = (f32[5,32,256]{2,1,0:T(8,128)S(1)}, f32[5,32,256]{2,1,0:T(8,128)S(1)}, u32[]{:S(2)}, u32[]{:S(2)}) collective-permute-start(f32[5,32,256]{2,1,0:T(8,128)S(1)} %fusion.185), channel_id=1, source_target_pairs={{4,0},{8,4},{12,8},{16,12},{20,16},{24,20},{28,24},{5,1},{9,5},{13... | collective-permute-start | bytes 491528 | tf_op jit(solution)/shard_map/while/body/eval_jaxpr/ppermute | solution.py:32
  103.1 5.6 %collective-permute-done.1 = f32[5,32,256]{2,1,0:T(8,128)S(1)} collective-permute-done((f32[5,32,256]{2,1,0:T(8,128)S(1)}, f32[5,32,256]{2,1,0:T(8,128)S(1)}, u32[]{:S(2)}, u32[]{:S(2)}) %collective-permute-start.1) | collective-permute-done | bytes 163872 | tf_op jit(solution)/shard_map/while/body/eval_jaxpr/ppermute | solution.py:32
  108.9 1.9 %collective-permute-start.1 = (f32[5,32,256]{2,1,0:T(8,128)S(1)}, f32[5,32,256]{2,1,0:T(8,128)S(1)}, u32[]{:S(2)}, u32[]{:S(2)}) collective-permute-start(f32[5,32,256]{2,1,0:T(8,128)S(1)} %fusion.185), channel_id=1, source_target_pairs={{4,0},{8,4},{12,8},{16,12},{20,16},{24,20},{28,24},{5,1},{9,5},{13... | collective-permute-start | bytes 491528 | tf_op jit(solution)/shard_map/while/body/eval_jaxpr/ppermute | solution.py:32
  110.8 5.6 %collective-permute-done.1 = f32[5,32,256]{2,1,0:T(8,128)S(1)} collective-permute-done((f32[5,32,256]{2,1,0:T(8,128)S(1)}, f32[5,32,256]{2,1,0:T(8,128)S(1)}, u32[]{:S(2)}, u32[]{:S(2)}) %collective-permute-start.1) | collective-permute-done | bytes 163872 | tf_op jit(solution)/shard_map/while/body/eval_jaxpr/ppermute | solution.py:32
  116.5 1.9 %collective-permute-start.1 = (f32[5,32,256]{2,1,0:T(8,128)S(1)}, f32[5,32,256]{2,1,0:T(8,128)S(1)}, u32[]{:S(2)}, u32[]{:S(2)}) collective-permute-start(f32[5,32,256]{2,1,0:T(8,128)S(1)} %fusion.185), channel_id=1, source_target_pairs={{4,0},{8,4},{12,8},{16,12},{20,16},{24,20},{28,24},{5,1},{9,5},{13... | collective-permute-start | bytes 491528 | tf_op jit(solution)/shard_map/while/body/eval_jaxpr/ppermute | solution.py:32
  118.5 5.6 %collective-permute-done.1 = f32[5,32,256]{2,1,0:T(8,128)S(1)} collective-permute-done((f32[5,32,256]{2,1,0:T(8,128)S(1)}, f32[5,32,256]{2,1,0:T(8,128)S(1)}, u32[]{:S(2)}, u32[]{:S(2)}) %collective-permute-start.1) | collective-permute-done | bytes 163872 | tf_op jit(solution)/shard_map/while/body/eval_jaxpr/ppermute | solution.py:32
  124.2 1.9 %collective-permute-start.1 = (f32[5,32,256]{2,1,0:T(8,128)S(1)}, f32[5,32,256]{2,1,0:T(8,128)S(1)}, u32[]{:S(2)}, u32[]{:S(2)}) collective-permute-start(f32[5,32,256]{2,1,0:T(8,128)S(1)} %fusion.185), channel_id=1, source_target_pairs={{4,0},{8,4},{12,8},{16,12},{20,16},{24,20},{28,24},{5,1},{9,5},{13... | collective-permute-start | bytes 491528 | tf_op jit(solution)/shard_map/while/body/eval_jaxpr/ppermute | solution.py:32
  126.1 5.6 %collective-permute-done.1 = f32[5,32,256]{2,1,0:T(8,128)S(1)} collective-permute-done((f32[5,32,256]{2,1,0:T(8,128)S(1)}, f32[5,32,256]{2,1,0:T(8,128)S(1)}, u32[]{:S(2)}, u32[]{:S(2)}) %collective-permute-start.1) | collective-permute-done | bytes 163872 | tf_op jit(solution)/shard_map/while/body/eval_jaxpr/ppermute | solution.py:32
  131.9 1.9 %collective-permute-start.1 = (f32[5,32,256]{2,1,0:T(8,128)S(1)}, f32[5,32,256]{2,1,0:T(8,128)S(1)}, u32[]{:S(2)}, u32[]{:S(2)}) collective-permute-start(f32[5,32,256]{2,1,0:T(8,128)S(1)} %fusion.185), channel_id=1, source_target_pairs={{4,0},{8,4},{12,8},{16,12},{20,16},{24,20},{28,24},{5,1},{9,5},{13... | collective-permute-start | bytes 491528 | tf_op jit(solution)/shard_map/while/body/eval_jaxpr/ppermute | solution.py:32
  133.8 5.6 %collective-permute-done.1 = f32[5,32,256]{2,1,0:T(8,128)S(1)} collective-permute-done((f32[5,32,256]{2,1,0:T(8,128)S(1)}, f32[5,32,256]{2,1,0:T(8,128)S(1)}, u32[]{:S(2)}, u32[]{:S(2)}) %collective-permute-start.1) | collective-permute-done | bytes 163872 | tf_op jit(solution)/shard_map/while/body/eval_jaxpr/ppermute | solution.py:32
  140.5 0.8 add_divide_fusion
  141.2 0.7 copy-done
  (131 shorter events, 6.9 us)
Async XLA Ops:
  2.0 6.5 %collective-permute-start.2 = (f32[2,8,7,256]{3,2,1,0:T(8,128)S(1)}, f32[2,8,7,256]{3,2,1,0:T(8,128)S(1)}, u32[]{:S(2)}, u32[]{:S(2)}) collective-permute-start(f32[2,8,7,256]{3,2,1,0:T(8,128)S(1)} %get-tuple-element.470), channel_id=1, source_target_pairs={{0,1},{1,2},{2,3},{4,5},{5,6},{6,7},{8,9},{9,10},{10,11},{12,13},{... | collective-permute-start | bytes 344072 | tf_op jit(solution)/shard_map/ppermute | solution.py:23
  5.2 5.7 %collective-permute-start.3 = (f32[2,8,7,256]{3,2,1,0:T(8,128)S(1)}, f32[2,8,7,256]{3,2,1,0:T(8,128)S(1)}, u32[]{:S(2)}, u32[]{:S(2)}) collective-permute-start(f32[2,8,7,256]{3,2,1,0:T(8,128)S(1)} %get-tuple-element.471), channel_id=1, source_target_pairs={{1,0},{2,1},{3,2},{5,4},{6,5},{7,6},{9,8},{10,9},{11,10},{13,12},{... | collective-permute-start | bytes 344072 | tf_op jit(solution)/shard_map/ppermute | solution.py:24
  27.7 7.4 %collective-permute-start = (f32[5,32,256]{2,1,0:T(8,128)S(1)}, f32[5,32,256]{2,1,0:T(8,128)S(1)}, u32[]{:S(2)}, u32[]{:S(2)}) collective-permute-start(f32[5,32,256]{2,1,0:T(8,128)S(1)} %fusion.180), channel_id=1, source_target_pairs={{0,4},{4,8},{8,12},{12,16},{16,20},{20,24},{24,28},{1,5},{5,9},{9,... | collective-permute-start | bytes 491528 | tf_op jit(solution)/shard_map/while/body/eval_jaxpr/ppermute | solution.py:32
  35.3 7.5 %collective-permute-start = (f32[5,32,256]{2,1,0:T(8,128)S(1)}, f32[5,32,256]{2,1,0:T(8,128)S(1)}, u32[]{:S(2)}, u32[]{:S(2)}) collective-permute-start(f32[5,32,256]{2,1,0:T(8,128)S(1)} %fusion.180), channel_id=1, source_target_pairs={{0,4},{4,8},{8,12},{12,16},{16,20},{20,24},{24,28},{1,5},{5,9},{9,... | collective-permute-start | bytes 491528 | tf_op jit(solution)/shard_map/while/body/eval_jaxpr/ppermute | solution.py:32
  43.0 7.5 %collective-permute-start = (f32[5,32,256]{2,1,0:T(8,128)S(1)}, f32[5,32,256]{2,1,0:T(8,128)S(1)}, u32[]{:S(2)}, u32[]{:S(2)}) collective-permute-start(f32[5,32,256]{2,1,0:T(8,128)S(1)} %fusion.180), channel_id=1, source_target_pairs={{0,4},{4,8},{8,12},{12,16},{16,20},{20,24},{24,28},{1,5},{5,9},{9,... | collective-permute-start | bytes 491528 | tf_op jit(solution)/shard_map/while/body/eval_jaxpr/ppermute | solution.py:32
  50.8 7.5 %collective-permute-start = (f32[5,32,256]{2,1,0:T(8,128)S(1)}, f32[5,32,256]{2,1,0:T(8,128)S(1)}, u32[]{:S(2)}, u32[]{:S(2)}) collective-permute-start(f32[5,32,256]{2,1,0:T(8,128)S(1)} %fusion.180), channel_id=1, source_target_pairs={{0,4},{4,8},{8,12},{12,16},{16,20},{20,24},{24,28},{1,5},{5,9},{9,... | collective-permute-start | bytes 491528 | tf_op jit(solution)/shard_map/while/body/eval_jaxpr/ppermute | solution.py:32
  58.5 7.5 %collective-permute-start = (f32[5,32,256]{2,1,0:T(8,128)S(1)}, f32[5,32,256]{2,1,0:T(8,128)S(1)}, u32[]{:S(2)}, u32[]{:S(2)}) collective-permute-start(f32[5,32,256]{2,1,0:T(8,128)S(1)} %fusion.180), channel_id=1, source_target_pairs={{0,4},{4,8},{8,12},{12,16},{16,20},{20,24},{24,28},{1,5},{5,9},{9,... | collective-permute-start | bytes 491528 | tf_op jit(solution)/shard_map/while/body/eval_jaxpr/ppermute | solution.py:32
  66.3 7.5 %collective-permute-start = (f32[5,32,256]{2,1,0:T(8,128)S(1)}, f32[5,32,256]{2,1,0:T(8,128)S(1)}, u32[]{:S(2)}, u32[]{:S(2)}) collective-permute-start(f32[5,32,256]{2,1,0:T(8,128)S(1)} %fusion.180), channel_id=1, source_target_pairs={{0,4},{4,8},{8,12},{12,16},{16,20},{20,24},{24,28},{1,5},{5,9},{9,... | collective-permute-start | bytes 491528 | tf_op jit(solution)/shard_map/while/body/eval_jaxpr/ppermute | solution.py:32
  74.0 7.5 %collective-permute-start = (f32[5,32,256]{2,1,0:T(8,128)S(1)}, f32[5,32,256]{2,1,0:T(8,128)S(1)}, u32[]{:S(2)}, u32[]{:S(2)}) collective-permute-start(f32[5,32,256]{2,1,0:T(8,128)S(1)} %fusion.180), channel_id=1, source_target_pairs={{0,4},{4,8},{8,12},{12,16},{16,20},{20,24},{24,28},{1,5},{5,9},{9,... | collective-permute-start | bytes 491528 | tf_op jit(solution)/shard_map/while/body/eval_jaxpr/ppermute | solution.py:32
  85.1 8.3 %collective-permute-start.1 = (f32[5,32,256]{2,1,0:T(8,128)S(1)}, f32[5,32,256]{2,1,0:T(8,128)S(1)}, u32[]{:S(2)}, u32[]{:S(2)}) collective-permute-start(f32[5,32,256]{2,1,0:T(8,128)S(1)} %fusion.185), channel_id=1, source_target_pairs={{4,0},{8,4},{12,8},{16,12},{20,16},{24,20},{28,24},{5,1},{9,5},{13... | collective-permute-start | bytes 491528 | tf_op jit(solution)/shard_map/while/body/eval_jaxpr/ppermute | solution.py:32
  93.5 7.5 %collective-permute-start.1 = (f32[5,32,256]{2,1,0:T(8,128)S(1)}, f32[5,32,256]{2,1,0:T(8,128)S(1)}, u32[]{:S(2)}, u32[]{:S(2)}) collective-permute-start(f32[5,32,256]{2,1,0:T(8,128)S(1)} %fusion.185), channel_id=1, source_target_pairs={{4,0},{8,4},{12,8},{16,12},{20,16},{24,20},{28,24},{5,1},{9,5},{13... | collective-permute-start | bytes 491528 | tf_op jit(solution)/shard_map/while/body/eval_jaxpr/ppermute | solution.py:32
  101.2 7.5 %collective-permute-start.1 = (f32[5,32,256]{2,1,0:T(8,128)S(1)}, f32[5,32,256]{2,1,0:T(8,128)S(1)}, u32[]{:S(2)}, u32[]{:S(2)}) collective-permute-start(f32[5,32,256]{2,1,0:T(8,128)S(1)} %fusion.185), channel_id=1, source_target_pairs={{4,0},{8,4},{12,8},{16,12},{20,16},{24,20},{28,24},{5,1},{9,5},{13... | collective-permute-start | bytes 491528 | tf_op jit(solution)/shard_map/while/body/eval_jaxpr/ppermute | solution.py:32
  108.9 7.5 %collective-permute-start.1 = (f32[5,32,256]{2,1,0:T(8,128)S(1)}, f32[5,32,256]{2,1,0:T(8,128)S(1)}, u32[]{:S(2)}, u32[]{:S(2)}) collective-permute-start(f32[5,32,256]{2,1,0:T(8,128)S(1)} %fusion.185), channel_id=1, source_target_pairs={{4,0},{8,4},{12,8},{16,12},{20,16},{24,20},{28,24},{5,1},{9,5},{13... | collective-permute-start | bytes 491528 | tf_op jit(solution)/shard_map/while/body/eval_jaxpr/ppermute | solution.py:32
  116.5 7.5 %collective-permute-start.1 = (f32[5,32,256]{2,1,0:T(8,128)S(1)}, f32[5,32,256]{2,1,0:T(8,128)S(1)}, u32[]{:S(2)}, u32[]{:S(2)}) collective-permute-start(f32[5,32,256]{2,1,0:T(8,128)S(1)} %fusion.185), channel_id=1, source_target_pairs={{4,0},{8,4},{12,8},{16,12},{20,16},{24,20},{28,24},{5,1},{9,5},{13... | collective-permute-start | bytes 491528 | tf_op jit(solution)/shard_map/while/body/eval_jaxpr/ppermute | solution.py:32
  124.2 7.5 %collective-permute-start.1 = (f32[5,32,256]{2,1,0:T(8,128)S(1)}, f32[5,32,256]{2,1,0:T(8,128)S(1)}, u32[]{:S(2)}, u32[]{:S(2)}) collective-permute-start(f32[5,32,256]{2,1,0:T(8,128)S(1)} %fusion.185), channel_id=1, source_target_pairs={{4,0},{8,4},{12,8},{16,12},{20,16},{24,20},{28,24},{5,1},{9,5},{13... | collective-permute-start | bytes 491528 | tf_op jit(solution)/shard_map/while/body/eval_jaxpr/ppermute | solution.py:32
  131.9 7.5 %collective-permute-start.1 = (f32[5,32,256]{2,1,0:T(8,128)S(1)}, f32[5,32,256]{2,1,0:T(8,128)S(1)}, u32[]{:S(2)}, u32[]{:S(2)}) collective-permute-start(f32[5,32,256]{2,1,0:T(8,128)S(1)} %fusion.185), channel_id=1, source_target_pairs={{4,0},{8,4},{12,8},{16,12},{20,16},{24,20},{28,24},{5,1},{9,5},{13... | collective-permute-start | bytes 491528 | tf_op jit(solution)/shard_map/while/body/eval_jaxpr/ppermute | solution.py:32
  141.2 0.7 copy-start
where the time goes:
time: 143 us; the launch traced here: 142 us
  waiting for transfers between devices  58.1 us (41%)
  starting transfers between devices  54.8 us (38%)
  other arithmetic  24.6 us (17%)
  local copies, waits for them, and re-layouts  1.5 us (1%)
    ppermute x14, waiting for transfers between devices, from_behind(): return lax.ppermute(shard, axis, pairs)  55.6 us
    ppermute x14, starting transfers between devices, from_behind(): return lax.ppermute(shard, axis, pairs)  50.3 us
    add x1, other arithmetic, body(): rowsum + taps_row[shift_row] * padded[:, :, shift_row:shift_row + row_cou...  10.3 us
    ppermute x1, starting transfers between devices, extended(): before = lax.ppermute(last, axis, up)  3.21 us
    add x12, other arithmetic, vec_add(): return (u[0] + v[0], u[1] + v[1])  2.97 us
  transfers between devices with their start and end apart: 16, of which 15 were waited for; matrix products, arithmetic and copies ran while one was open for 1% of the time, Pallas kernels for 0%

commit v1 on v0

v1 whole, which is shorter than its diff:
```python
import functools
import math

import jax
import jax.numpy as jnp
from jax import lax
from jax.experimental import pallas as pl
from jax.experimental.pallas import tpu as pltpu
from jax.sharding import PartitionSpec as P

RADIUS = 7
SCALE_T = 64
SUB = 8
LANES = 128
SAVED = 7

sigma_cells = 3.0
prior_var = 4.0


def dynamics():
    rate = math.sqrt(3.0) / SCALE_T
    factor = math.exp(-rate)
    a, b, c, d = (
        factor * (1.0 + rate),
        factor,
        -factor * rate * rate,
        factor * (1.0 - rate),
    )
    p0, p1 = prior_var, prior_var * rate * rate
    noise = (
        p0 - (a * a * p0 + b * b * p1),
        -(a * c * p0 + b * d * p1),
        p1 - (c * c * p0 + d * d * p1),
    )
    return (a, b, c, d), (p0, p1), noise


def taps():
    raw = [math.exp(-o * o / (2.0 * sigma_cells**2)) for o in range(-RADIUS, RADIUS + 1)]
    total = sum(raw)
    return [r / total for r in raw], total


def kernel(tm_count, space_count, hits, misses, occ, spr, chan, horiz, window, send, recv, saved,
           back, landed, halo_send, halo_recv, go_send, go_recv, ret_send, ret_recv):
    frames, rows, cols = hits.shape
    halves = cols // LANES
    chunks = (rows // SUB) * halves
    stride = tm_count // chunks
    me = lax.axis_index("tm")
    tile = lax.axis_index("space")
    mine = me // stride
    (ta, tb, tc, td), (prior0, prior1), (q00, q01, q11) = dynamics()
    weights, total = taps()
    has_up = tile > 0
    has_down = tile < space_count - 1
    barrier = pltpu.get_barrier_semaphore()

    def greet(k, carry):
        pl.semaphore_signal(barrier, inc=1, device_id={"tm": (me + k) % tm_count})
        return carry

    lax.fori_loop(1, tm_count, greet, 0)

    @pl.when(has_up)
    def _():
        pl.semaphore_signal(barrier, inc=1, device_id={"space": tile - 1})

    @pl.when(has_down)
    def _():
        pl.semaphore_signal(barrier, inc=1, device_id={"space": tile + 1})

    own = pl.ds(SUB, rows)

    def observe(f, carry):
        h, m = hits[f], misses[f]
        hp = h.astype(jnp.float32) + 1.0
        mp = m.astype(jnp.float32) + 1.0
        both = hp + mp
        weight = (h + m).astype(jnp.float32) * hp * mp / (both * both)
        chan[0, f, own, :] = weight * jnp.log(hp / mp)
        chan[1, f, own, :] = weight
        return carry

    lax.fori_loop(0, frames, observe, 0)

    @pl.when(jnp.logical_not(has_up))
    def _():
        chan[:, :, 0:SUB, :] = jnp.zeros((2, frames, SUB, cols), jnp.float32)

    @pl.when(jnp.logical_not(has_down))
    def _():
        chan[:, :, SUB + rows :, :] = jnp.zeros((2, frames, SUB, cols), jnp.float32)

    neighbours = has_up.astype(jnp.int32) + has_down.astype(jnp.int32)
    pl.semaphore_wait(barrier, tm_count - 1 + neighbours)

    to_down = pltpu.make_async_remote_copy(
        src_ref=chan.at[:, :, pl.ds(rows, SUB), :],
        dst_ref=chan.at[:, :, pl.ds(0, SUB), :],
        send_sem=halo_send.at[0], recv_sem=halo_recv.at[0],
        device_id={"space": tile + 1})
    to_up = pltpu.make_async_remote_copy(
        src_ref=chan.at[:, :, pl.ds(SUB, SUB), :],
        dst_ref=chan.at[:, :, pl.ds(SUB + rows, SUB), :],
        send_sem=halo_send.at[1], recv_sem=halo_recv.at[1],
        device_id={"space": tile - 1})

    @pl.when(has_down)
    def _():
        to_down.start()

    @pl.when(has_up)
    def _():
        to_up.start()

    offset = (lax.broadcasted_iota(jnp.int32, (cols, cols), 0)
              - lax.broadcasted_iota(jnp.int32, (cols, cols), 1))
    far = offset.astype(jnp.float32)
    band = jnp.where(jnp.abs(offset) <= RADIUS,
                     jnp.exp(-far * far / (2.0 * sigma_cells**2)) / total, 0.0)

    def across(start, size):
        flat = chan[:, :, start : start + size, :].reshape(2 * frames * size, cols)
        out = jnp.dot(flat, band, precision=lax.Precision.HIGHEST,
                      preferred_element_type=jnp.float32)
        horiz[:, :, start : start + size, :] = out.reshape(2, frames, size, cols)

    across(SUB, rows)

    @pl.when(has_up)
    def _():
        to_down.wait_recv()

    @pl.when(has_down)
    def _():
        to_up.wait_recv()

    across(0, SUB)
    across(SUB + rows, SUB)

    def down_chunk(j):
        row0 = pl.multiple_of((j // halves) * SUB, SUB)
        col0 = pl.multiple_of((j % halves) * LANES, LANES)
        window[...] = horiz[:, :, pl.ds(row0, 3 * SUB), pl.ds(col0, LANES)]

        def at(s):
            first = SUB - RADIUS + s
            return window[:, :, first : first + SUB, :]

        out = weights[RADIUS] * at(RADIUS)
        for s in range(RADIUS):
            out = out + weights[s] * (at(s) + at(2 * RADIUS - s))
        return out

    def go_copy(j):
        return pltpu.make_async_remote_copy(
            src_ref=send.at[j], dst_ref=recv.at[me], send_sem=go_send.at[j],
            recv_sem=go_recv.at[me], device_id={"tm": j * stride})

    def scatter(k, carry):
        j = (mine + k) % chunks
        send[j] = down_chunk(j)
        go_copy(j).start()
        return carry

    lax.fori_loop(1, chunks, scatter, 0)
    if stride == 1:
        recv[me] = down_chunk(mine)
    else:
        send[mine] = down_chunk(mine)

        @pl.when(me % stride == 0)
        def _():
            recv[me] = send[mine]

        @pl.when(me % stride != 0)
        def _():
            go_copy(mine).start()

    def back_copy(i):
        return pltpu.make_async_remote_copy(
            src_ref=back.at[i], dst_ref=landed.at[mine], send_sem=ret_send.at[i],
            recv_sem=ret_recv.at[mine], device_id={"tm": i})

    def smooth():
        def forward(i, state):
            @pl.when(i != me)
            def _():
                pltpu.make_async_remote_copy(
                    src_ref=send.at[0], dst_ref=recv.at[i], send_sem=go_send.at[0],
                    recv_sem=go_recv.at[i], device_id={"tm": i}).wait_recv()

            m0, m1, p00, p01, p11 = state
            for f in range(frames):
                num, den = recv[i, 0, f], recv[i, 1, f]
                inv = 1.0 / (1.0 + p00 * den)
                w = den * inv
                e = (num - den * m0) * inv
                k1 = p01 * w
                m0, m1 = m0 + p00 * e, m1 + p01 * e
                p11 = p11 - k1 * p01
                p00, p01 = p00 * inv, p01 * inv
                for slot, value in enumerate((inv, w, e, k1, m0, p00, p01)):
                    saved[i, f, slot] = value
                m0, m1 = ta * m0 + tb * m1, tc * m0 + td * m1
                p00, p01, p11 = (
                    (ta * ta) * p00 + (2.0 * ta * tb) * p01 + ((tb * tb) * p11 + q00),
                    (ta * tc) * p00 + (ta * td + tb * tc) * p01 + ((tb * td) * p11 + q01),
                    (tc * tc) * p00 + (2.0 * tc * td) * p01 + ((td * td) * p11 + q11),
                )
            return m0, m1, p00, p01, p11

        zero = jnp.zeros((SUB, LANES), jnp.float32)
        lax.fori_loop(0, tm_count, forward, (zero, zero, zero + prior0, zero, zero + prior1))

        def backward(n, state):
            i = tm_count - 1 - n
            u0, u1, n00, n01, n11 = state
            for f in reversed(range(frames)):
                inv, w, e, k1, m0, p00, p01 = (saved[i, f, slot] for slot in range(SAVED))
                mean = m0 + p00 * u0 + p01 * u1
                back[i, 0, f] = 1.0 / (1.0 + jnp.exp(-mean))
                back[i, 1, f] = p00 - (
                    p00 * p00 * n00 + 2.0 * (p00 * p01) * n01 + p01 * p01 * n11)
                r0 = e + inv * u0 - k1 * u1
                l00 = w + (inv * inv) * n00 - (2.0 * inv * k1) * n01 + (k1 * k1) * n11
                l01 = inv * n01 - k1 * n11
                u0, u1 = ta * r0 + tc * u1, tb * r0 + td * u1
                n00, n01, n11 = (
                    (ta * ta) * l00 + ((2.0 * ta * tc) * l01 + (tc * tc) * n11),
                    (ta * tb) * l00 + ((ta * td + tb * tc) * l01 + (tc * td) * n11),
                    (tb * tb) * l00 + ((2.0 * tb * td) * l01 + (td * td) * n11),
                )

            @pl.when(i != me)
            def _():
                back_copy(i).start()

            @pl.when(i == me)
            def _():
                landed[mine] = back[i]

            return u0, u1, n00, n01, n11

        lax.fori_loop(0, tm_count, backward, (zero,) * 5)

    if stride == 1:
        smooth()
    else:
        pl.when(me % stride == 0)(smooth)

    def place(k, carry):
        j = (mine + k) % chunks

        @pl.when(j * stride != me)
        def _():
            pltpu.make_async_remote_copy(
                src_ref=back.at[0], dst_ref=landed.at[j], send_sem=ret_send.at[0],
                recv_sem=ret_recv.at[j], device_id={"tm": j * stride}).wait_recv()

        row0 = pl.multiple_of((j // halves) * SUB, SUB)
        col0 = pl.multiple_of((j % halves) * LANES, LANES)
        occ[:, pl.ds(row0, SUB), pl.ds(col0, LANES)] = landed[j, 0]
        spr[:, pl.ds(row0, SUB), pl.ds(col0, LANES)] = landed[j, 1]
        return carry

    lax.fori_loop(0, chunks, place, 0)

    @pl.when(has_down)
    def _():
        to_down.wait_send()

    @pl.when(has_up)
    def _():
        to_up.wait_send()

    def sent(j, carry):
        @pl.when(j * stride != me)
        def _():
            go_copy(j).wait_send()

        return carry

    lax.fori_loop(0, chunks, sent, 0)

    def returned(i, carry):
        @pl.when(jnp.logical_and(i != me, me % stride == 0))
        def _():
            back_copy(i).wait_send()

        return carry

    lax.fori_loop(0, tm_count, returned, 0)


def solution(mesh):
    tm_count, space_count = mesh.shape["tm"], mesh.shape["space"]

    def body(hits, misses):
        frames, rows, cols = hits.shape
        chunks = (rows // SUB) * (cols // LANES)
        cells = (SUB, LANES)
        vmem = pl.BlockSpec(memory_space=pltpu.VMEM)
        out = jax.ShapeDtypeStruct(hits.shape, jnp.float32)
        return pl.pallas_call(
            functools.partial(kernel, tm_count, space_count),
            out_shape=(out, out),
            in_specs=[vmem, vmem],
            out_specs=(vmem, vmem),
            scratch_shapes=[
                pltpu.VMEM((2, frames, rows + 2 * SUB, cols), jnp.float32),
                pltpu.VMEM((2, frames, rows + 2 * SUB, cols), jnp.float32),
                pltpu.VMEM((2, frames, 3 * SUB, LANES), jnp.float32),
                pltpu.VMEM((chunks, 2, frames) + cells, jnp.float32),
                pltpu.VMEM((tm_count, 2, frames) + cells, jnp.float32),
                pltpu.VMEM((tm_count, frames, SAVED) + cells, jnp.float32),
                pltpu.VMEM((tm_count, 2, frames) + cells, jnp.float32),
                pltpu.VMEM((chunks, 2, frames) + cells, jnp.float32),
                pltpu.SemaphoreType.DMA((2,)),
                pltpu.SemaphoreType.DMA((2,)),
                pltpu.SemaphoreType.DMA((chunks,)),
                pltpu.SemaphoreType.DMA((tm_count,)),
                pltpu.SemaphoreType.DMA((tm_count,)),
                pltpu.SemaphoreType.DMA((chunks,)),
            ],
            compiler_params=pltpu.CompilerParams(
                collective_id=0, has_side_effects=True, vmem_limit_bytes=48 * 1024 * 1024),
        )(hits, misses)

    placed = P("tm", "space", None)
    return jax.shard_map(body, mesh=mesh, in_specs=(placed, placed),
                         out_specs=(placed, placed), check_vma=False)
```

time: 143 us -> 31 us (0.22)
  the two profiles are of different devices: /device:TPU:3 before, /device:TPU:0 now
where the time goes in v1:
time: 31 us; the launch traced here: 30.8 us
  Pallas kernels  26.9 us (87%)
  local copies, waits for them, and re-layouts  3.3 us (11%)
  between operations  0.65 us (2%)
    pallas_call x1, Pallas kernels, body(): pl.pallas_call(functools.partial(kernel, tm_count, space_count), out_shap...  26.9 us
    unnamed x6, local copies, waits for them, and re-layouts  3.3 us

profile of v1, /device:TPU:0, one launch (start us, length us, event | category | flops | bytes accessed | tf_op | source)
XLA Modules:
  0.0 30.8 jit_solution(2652895527901782526)
XLA Ops:
  0.6 0.0 copy-start
  0.6 0.9 %copy-done = s32[8,32,256]{2,1,0:T(8,128)S(1)} copy-done((s32[8,32,256]{2,1,0:T(8,128)S(1)}, s32[8,32,256]{2,1,0:T(8,128)}, u32[]{:S(2)}) %copy-start) | copy-done | bytes 262168
  1.6 0.0 copy-start.1
  1.6 0.9 %copy-done.1 = s32[8,32,256]{2,1,0:T(8,128)S(1)} copy-done((s32[8,32,256]{2,1,0:T(8,128)S(1)}, s32[8,32,256]{2,1,0:T(8,128)}, u32[]{:S(2)}) %copy-start.1) | copy-done | bytes 262168
  2.5 26.9 %shard_map.41 = (f32[8,32,256]{2,1,0:T(8,128)S(1)}, f32[8,32,256]{2,1,0:T(8,128)S(1)}) custom-call(s32[8,32,256]{2,1,0:T(8,128)S(1)} %copy-done, s32[8,32,256]{2,1,0:T(8,128)S(1)} %copy-done.1), custom_call_target="tpu_custom_call" | custom-call | tf_op jit(solution)/shard_map/pallas_call | solution.py:307
  29.4 0.7 %copy.6 = f32[8,32,256]{2,1,0:T(8,128)} copy(f32[8,32,256]{2,1,0:T(8,128)S(1)} %get-tuple-element.4) | data formatting | bytes 524288
  30.1 0.7 %copy.7 = f32[8,32,256]{2,1,0:T(8,128)} copy(f32[8,32,256]{2,1,0:T(8,128)S(1)} %get-tuple-element.5) | data formatting | bytes 524288
Async XLA Ops:
  0.6 1.0 %copy-start = (s32[8,32,256]{2,1,0:T(8,128)S(1)}, s32[8,32,256]{2,1,0:T(8,128)}, u32[]{:S(2)}) copy-start(s32[8,32,256]{2,1,0:T(8,128)} %hits.1) | copy-start | bytes 786436
  1.6 0.9 %copy-start.1 = (s32[8,32,256]{2,1,0:T(8,128)S(1)}, s32[8,32,256]{2,1,0:T(8,128)}, u32[]{:S(2)}) copy-start(s32[8,32,256]{2,1,0:T(8,128)} %misses.1) | copy-start | bytes 786436

commit v2 on v1

--- a/solution.py
+++ b/solution.py
@@ -42,9 +42,14 @@
     return [r / total for r in raw], total
 
 
-def kernel(tm_count, space_count, hits, misses, occ, spr, chan, horiz, window, send, recv, saved,
-           back, landed, halo_send, halo_recv, go_send, go_recv, ret_send, ret_recv):
+def kernel(tm_count, space_count, hits_hbm, misses_hbm, occ, spr, hits, misses, chan, horiz, window, send, recv, saved,
+           back, landed, halo_send, halo_recv, go_send, go_recv, ret_send, ret_recv, load):
+    load_hits = pltpu.make_async_copy(hits_hbm, hits, load.at[0])
+    load_misses = pltpu.make_async_copy(misses_hbm, misses, load.at[1])
+    load_hits.start()
+    load_misses.start()
     frames, rows, cols = hits.shape
+    groups = rows // SUB
     halves = cols // LANES
     chunks = (rows // SUB) * halves
     stride = tm_count // chunks
@@ -72,6 +77,8 @@
         pl.semaphore_signal(barrier, inc=1, device_id={"space": tile + 1})
 
     own = pl.ds(SUB, rows)
+    load_hits.wait()
+    load_misses.wait()
 
     def observe(f, carry):
         h, m = hits[f], misses[f]
@@ -127,22 +134,15 @@
                       preferred_element_type=jnp.float32)
         horiz[:, :, start : start + size, :] = out.reshape(2, frames, size, cols)
 
-    across(SUB, rows)
-
-    @pl.when(has_up)
-    def _():
-        to_down.wait_recv()
-
-    @pl.when(has_down)
-    def _():
-        to_up.wait_recv()
-
-    across(0, SUB)
-    across(SUB + rows, SUB)
+    def corner(j):
+        pair, edge = j // 2, j % 2
+        side = pair // halves
+        group = edge * side * (groups - 1) + (1 - edge) * (1 + side)
+        return (pl.multiple_of(group * SUB, SUB),
+                pl.multiple_of((pair % halves) * LANES, LANES))
 
     def down_chunk(j):
-        row0 = pl.multiple_of((j // halves) * SUB, SUB)
-        col0 = pl.multiple_of((j % halves) * LANES, LANES)
+        row0, col0 = corner(j)
         window[...] = horiz[:, :, pl.ds(row0, 3 * SUB), pl.ds(col0, LANES)]
 
         def at(s):
@@ -159,25 +159,38 @@
             src_ref=send.at[j], dst_ref=recv.at[me], send_sem=go_send.at[j],
             recv_sem=go_recv.at[me], device_id={"tm": j * stride})
 
-    def scatter(k, carry):
-        j = (mine + k) % chunks
-        send[j] = down_chunk(j)
-        go_copy(j).start()
-        return carry
-
-    lax.fori_loop(1, chunks, scatter, 0)
-    if stride == 1:
-        recv[me] = down_chunk(mine)
-    else:
-        send[mine] = down_chunk(mine)
-
-        @pl.when(me % stride == 0)
-        def _():
-            recv[me] = send[mine]
-
-        @pl.when(me % stride != 0)
-        def _():
-            go_copy(mine).start()
+    def scatter(edge):
+        def step(k, carry):
+            pairs = chunks // 2
+            j = 2 * ((mine // 2 + k * (1 + 2 * (mine % 2))) % pairs) + edge
+            send[j] = down_chunk(j)
+
+            @pl.when(j * stride != me)
+            def _():
+                go_copy(j).start()
+
+            @pl.when(j * stride == me)
+            def _():
+                recv[me] = send[j]
+
+            return carry
+
+        lax.fori_loop(1, chunks // 2 + 1, step, 0)
+
+    across(SUB, rows)
+    scatter(0)
+
+    @pl.when(has_up)
+    def _():
+        to_down.wait_recv()
+
+    @pl.when(has_down)
+    def _():
+        to_up.wait_recv()
+
+    across(0, SUB)
+    across(SUB + rows, SUB)
+    scatter(1)
 
     def back_copy(i):
         return pltpu.make_async_remote_copy(
@@ -234,17 +247,16 @@
                     (tb * tb) * l00 + ((2.0 * tb * td) * l01 + (td * td) * n11),
                 )
 
-            @pl.when(i != me)
-            def _():
-                back_copy(i).start()
-
-            @pl.when(i == me)
-            def _():
-                landed[mine] = back[i]
-
             return u0, u1, n00, n01, n11
 
         lax.fori_loop(0, tm_count, backward, (zero,) * 5)
+
+        def give(k, carry):
+            back_copy((me + k) % tm_count).start()
+            return carry
+
+        lax.fori_loop(1, tm_count, give, 0)
+        landed[mine] = back[me]
 
     if stride == 1:
         smooth()
@@ -260,8 +272,7 @@
                 src_ref=back.at[0], dst_ref=landed.at[j], send_sem=ret_send.at[0],
                 recv_sem=ret_recv.at[j], device_id={"tm": j * stride}).wait_recv()
 
-        row0 = pl.multiple_of((j // halves) * SUB, SUB)
-        col0 = pl.multiple_of((j % halves) * LANES, LANES)
+        row0, col0 = corner(j)
         occ[:, pl.ds(row0, SUB), pl.ds(col0, LANES)] = landed[j, 0]
         spr[:, pl.ds(row0, SUB), pl.ds(col0, LANES)] = landed[j, 1]
         return carry
@@ -307,9 +318,11 @@
         return pl.pallas_call(
             functools.partial(kernel, tm_count, space_count),
             out_shape=(out, out),
-            in_specs=[vmem, vmem],
+            in_specs=[pl.BlockSpec(memory_space=pltpu.HBM)] * 2,
             out_specs=(vmem, vmem),
             scratch_shapes=[
+                pltpu.VMEM(hits.shape, jnp.int32),
+                pltpu.VMEM(hits.shape, jnp.int32),
                 pltpu.VMEM((2, frames, rows + 2 * SUB, cols), jnp.float32),
                 pltpu.VMEM((2, frames, rows + 2 * SUB, cols), jnp.float32),
                 pltpu.VMEM((2, frames, 3 * SUB, LANES), jnp.float32),
@@ -324,6 +337,7 @@
                 pltpu.SemaphoreType.DMA((tm_count,)),
                 pltpu.SemaphoreType.DMA((tm_count,)),
                 pltpu.SemaphoreType.DMA((chunks,)),
+                pltpu.SemaphoreType.DMA((2,)),
             ],
             compiler_params=pltpu.CompilerParams(
                 collective_id=0, has_side_effects=True, vmem_limit_bytes=48 * 1024 * 1024),

time: 31 us -> 24.5 us (0.79)
  the two profiles are of different devices: /device:TPU:0 before, /device:TPU:1 now
where the time goes in v2:
time: 24.5 us; the launch traced here: 24.3 us
  Pallas kernels  20.4 us (83%)
  local copies, waits for them, and re-layouts  3.3 us (13%)
  between operations  0.65 us (3%)
    pallas_call x1, Pallas kernels, body(): pl.pallas_call(functools.partial(kernel, tm_count, space_count), out_shap...  20.4 us
    unnamed x6, local copies, waits for them, and re-layouts  3.3 us

profile of v2, /device:TPU:1, one launch (start us, length us, event | category | flops | bytes accessed | tf_op | source)
XLA Modules:
  0.0 24.3 jit_solution(13054617540851225788)
XLA Ops:
  0.6 0.0 copy-start
  0.6 0.9 %copy-done = s32[8,32,256]{2,1,0:T(8,128)S(1)} copy-done((s32[8,32,256]{2,1,0:T(8,128)S(1)}, s32[8,32,256]{2,1,0:T(8,128)}, u32[]{:S(2)}) %copy-start) | copy-done | bytes 262168
  1.6 0.0 copy-start.1
  1.6 0.9 %copy-done.1 = s32[8,32,256]{2,1,0:T(8,128)S(1)} copy-done((s32[8,32,256]{2,1,0:T(8,128)S(1)}, s32[8,32,256]{2,1,0:T(8,128)}, u32[]{:S(2)}) %copy-start.1) | copy-done | bytes 262168
  2.5 20.4 %shard_map.41 = (f32[8,32,256]{2,1,0:T(8,128)S(1)}, f32[8,32,256]{2,1,0:T(8,128)S(1)}) custom-call(s32[8,32,256]{2,1,0:T(8,128)S(1)} %copy-done, s32[8,32,256]{2,1,0:T(8,128)S(1)} %copy-done.1), custom_call_target="tpu_custom_call" | custom-call | tf_op jit(solution)/shard_map/pallas_call | solution.py:318
  22.9 0.7 %copy.6 = f32[8,32,256]{2,1,0:T(8,128)} copy(f32[8,32,256]{2,1,0:T(8,128)S(1)} %get-tuple-element.4) | data formatting | bytes 524288
  23.6 0.7 %copy.7 = f32[8,32,256]{2,1,0:T(8,128)} copy(f32[8,32,256]{2,1,0:T(8,128)S(1)} %get-tuple-element.5) | data formatting | bytes 524288
Async XLA Ops:
  0.6 1.0 %copy-start = (s32[8,32,256]{2,1,0:T(8,128)S(1)}, s32[8,32,256]{2,1,0:T(8,128)}, u32[]{:S(2)}) copy-start(s32[8,32,256]{2,1,0:T(8,128)} %hits_hbm.1) | copy-start | bytes 786436
  1.6 0.9 %copy-start.1 = (s32[8,32,256]{2,1,0:T(8,128)S(1)}, s32[8,32,256]{2,1,0:T(8,128)}, u32[]{:S(2)}) copy-start(s32[8,32,256]{2,1,0:T(8,128)} %misses_hbm.1) | copy-start | bytes 786436

commit v3 on v2

--- a/solution.py
+++ b/solution.py
@@ -42,8 +42,30 @@
     return [r / total for r in raw], total
 
 
-def kernel(tm_count, space_count, hits_hbm, misses_hbm, occ, spr, hits, misses, chan, horiz, window, send, recv, saved,
-           back, landed, halo_send, halo_recv, go_send, go_recv, ret_send, ret_recv, load):
+def corner(j, groups, halves):
+    pair, edge = j // 2, j % 2
+    side = pair // halves
+    group = edge * side * (groups - 1) + (1 - edge) * (1 + side)
+    return group * SUB, (pair % halves) * LANES
+
+
+def spread_out(landed, occ, spr, sems):
+    groups, halves = occ.shape[1] // SUB, occ.shape[2] // LANES
+    copies = []
+    for j in range(groups * halves):
+        row0, col0 = corner(j, groups, halves)
+        for k, out in enumerate((occ, spr)):
+            copies.append(pltpu.make_async_copy(
+                landed.at[j, k], out.at[:, row0 : row0 + SUB, col0 : col0 + LANES],
+                sems.at[j, k]))
+    for copy in copies:
+        copy.start()
+    for copy in copies:
+        copy.wait()
+
+
+def kernel(tm_count, space_count, hits_hbm, misses_hbm, landed, hits, misses, chan, horiz,
+           window, send, recv, saved, back, halo_send, halo_recv, go_send, go_recv, ret_send, ret_recv, load):
     load_hits = pltpu.make_async_copy(hits_hbm, hits, load.at[0])
     load_misses = pltpu.make_async_copy(misses_hbm, misses, load.at[1])
     load_hits.start()
@@ -128,21 +150,20 @@
     band = jnp.where(jnp.abs(offset) <= RADIUS,
                      jnp.exp(-far * far / (2.0 * sigma_cells**2)) / total, 0.0)
 
+    band_high = band.astype(jnp.bfloat16)
+    band_low = (band - band_high.astype(jnp.float32)).astype(jnp.bfloat16)
+
     def across(start, size):
         flat = chan[:, :, start : start + size, :].reshape(2 * frames * size, cols)
-        out = jnp.dot(flat, band, precision=lax.Precision.HIGHEST,
-                      preferred_element_type=jnp.float32)
+        high = flat.astype(jnp.bfloat16)
+        low = (flat - high.astype(jnp.float32)).astype(jnp.bfloat16)
+        dot = functools.partial(jnp.dot, preferred_element_type=jnp.float32)
+        out = dot(high, band_high) + (dot(low, band_high) + dot(high, band_low))
         horiz[:, :, start : start + size, :] = out.reshape(2, frames, size, cols)
 
-    def corner(j):
-        pair, edge = j // 2, j % 2
-        side = pair // halves
-        group = edge * side * (groups - 1) + (1 - edge) * (1 + side)
-        return (pl.multiple_of(group * SUB, SUB),
-                pl.multiple_of((pair % halves) * LANES, LANES))
-
     def down_chunk(j):
-        row0, col0 = corner(j)
+        row0, col0 = corner(j, groups, halves)
+        row0, col0 = pl.multiple_of(row0, SUB), pl.multiple_of(col0, LANES)
         window[...] = horiz[:, :, pl.ds(row0, 3 * SUB), pl.ds(col0, LANES)]
 
         def at(s):
@@ -272,9 +293,6 @@
                 src_ref=back.at[0], dst_ref=landed.at[j], send_sem=ret_send.at[0],
                 recv_sem=ret_recv.at[j], device_id={"tm": j * stride}).wait_recv()
 
-        row0, col0 = corner(j)
-        occ[:, pl.ds(row0, SUB), pl.ds(col0, LANES)] = landed[j, 0]
-        spr[:, pl.ds(row0, SUB), pl.ds(col0, LANES)] = landed[j, 1]
         return carry
 
     lax.fori_loop(0, chunks, place, 0)
@@ -315,11 +333,11 @@
         cells = (SUB, LANES)
         vmem = pl.BlockSpec(memory_space=pltpu.VMEM)
         out = jax.ShapeDtypeStruct(hits.shape, jnp.float32)
-        return pl.pallas_call(
+        landed = pl.pallas_call(
             functools.partial(kernel, tm_count, space_count),
-            out_shape=(out, out),
+            out_shape=jax.ShapeDtypeStruct((chunks, 2, frames) + cells, jnp.float32),
             in_specs=[pl.BlockSpec(memory_space=pltpu.HBM)] * 2,
-            out_specs=(vmem, vmem),
+            out_specs=vmem,
             scratch_shapes=[
                 pltpu.VMEM(hits.shape, jnp.int32),
                 pltpu.VMEM(hits.shape, jnp.int32),
@@ -330,7 +348,6 @@
                 pltpu.VMEM((tm_count, 2, frames) + cells, jnp.float32),
                 pltpu.VMEM((tm_count, frames, SAVED) + cells, jnp.float32),
                 pltpu.VMEM((tm_count, 2, frames) + cells, jnp.float32),
-                pltpu.VMEM((chunks, 2, frames) + cells, jnp.float32),
                 pltpu.SemaphoreType.DMA((2,)),
                 pltpu.SemaphoreType.DMA((2,)),
                 pltpu.SemaphoreType.DMA((chunks,)),
@@ -342,6 +359,15 @@
             compiler_params=pltpu.CompilerParams(
                 collective_id=0, has_side_effects=True, vmem_limit_bytes=48 * 1024 * 1024),
         )(hits, misses)
+        hbm = pl.BlockSpec(memory_space=pltpu.HBM)
+        return pl.pallas_call(
+            spread_out,
+            out_shape=(out, out),
+            in_specs=[vmem],
+            out_specs=(hbm, hbm),
+            scratch_shapes=[pltpu.SemaphoreType.DMA((chunks, 2))],
+            compiler_params=pltpu.CompilerParams(vmem_limit_bytes=8 * 1024 * 1024),
+        )(landed)
 
     placed = P("tm", "space", None)
     return jax.shard_map(body, mesh=mesh, in_specs=(placed, placed),

time: 24.5 us -> 23.7 us (0.967)
  local copies, waits for them, and re-layouts: 3.3 us -> 1.89 us
  Pallas kernels: 20.4 us -> 21 us
    unnamed x6 -> x4, local copies, waits for them, and re-layouts: 3.3 us -> 1.89 us
    pallas_call x0 -> x1, Pallas kernels: none -> 0.92 us  [body(): pl.pallas_call(spread_out, out_shape=(out, out), in_specs=[vmem], out_spe...]
    pallas_call x1, Pallas kernels: 20.4 us -> 20.1 us  [body(): pl.pallas_call(functools.partial(kernel, tm_count, space_count), out_shap...]
where the time goes in v3:
time: 23.7 us; the launch traced here: 23.5 us
  Pallas kernels  21 us (89%)
  local copies, waits for them, and re-layouts  1.89 us (8%)
  between operations  0.65 us (3%)
    pallas_call x1, Pallas kernels, body(): pl.pallas_call(functools.partial(kernel, tm_count, space_count), out_shap...  20.1 us
    unnamed x4, local copies, waits for them, and re-layouts  1.89 us
    pallas_call x1, Pallas kernels, body(): pl.pallas_call(spread_out, out_shape=(out, out), in_specs=[vmem], out_spe...  0.92 us

profile of v3, /device:TPU:1, one launch (start us, length us, event | category | flops | bytes accessed | tf_op | source)
XLA Modules:
  0.0 23.5 jit_solution(14027461243825692926)
XLA Ops:
  0.6 0.0 copy-start
  0.6 0.9 %copy-done = s32[8,32,256]{2,1,0:T(8,128)S(1)} copy-done((s32[8,32,256]{2,1,0:T(8,128)S(1)}, s32[8,32,256]{2,1,0:T(8,128)}, u32[]{:S(2)}) %copy-start) | copy-done | bytes 262168
  1.6 0.0 copy-start.1
  1.6 0.9 %copy-done.1 = s32[8,32,256]{2,1,0:T(8,128)S(1)} copy-done((s32[8,32,256]{2,1,0:T(8,128)S(1)}, s32[8,32,256]{2,1,0:T(8,128)}, u32[]{:S(2)}) %copy-start.1) | copy-done | bytes 262168
  2.5 20.1 %shard_map.41.landed = f32[8,2,8,8,128]{4,3,2,1,0:T(8,128)S(1)} custom-call(s32[8,32,256]{2,1,0:T(8,128)S(1)} %copy-done, s32[8,32,256]{2,1,0:T(8,128)S(1)} %copy-done.1), custom_call_target="tpu_custom_call" | custom-call | tf_op jit(solution)/shard_map/pallas_call | solution.py:336
  22.6 0.9 %shard_map.42 = (f32[8,32,256]{2,1,0:T(8,128)}, f32[8,32,256]{2,1,0:T(8,128)}) custom-call(f32[8,2,8,8,128]{4,3,2,1,0:T(8,128)S(1)} %shard_map.41.landed), custom_call_target="tpu_custom_call" | custom-call | tf_op jit(solution)/shard_map/pallas_call | solution.py:363
Async XLA Ops:
  0.6 1.0 %copy-start = (s32[8,32,256]{2,1,0:T(8,128)S(1)}, s32[8,32,256]{2,1,0:T(8,128)}, u32[]{:S(2)}) copy-start(s32[8,32,256]{2,1,0:T(8,128)} %hits_hbm.1) | copy-start | bytes 786436
  1.6 0.9 %copy-start.1 = (s32[8,32,256]{2,1,0:T(8,128)S(1)}, s32[8,32,256]{2,1,0:T(8,128)}, u32[]{:S(2)}) copy-start(s32[8,32,256]{2,1,0:T(8,128)} %misses_hbm.1) | copy-start | bytes 786436

commit v4 on v3

--- a/solution.py
+++ b/solution.py
@@ -183,7 +183,7 @@
     def scatter(edge):
         def step(k, carry):
             pairs = chunks // 2
-            j = 2 * ((mine // 2 + k * (1 + 2 * (mine % 2))) % pairs) + edge
+            j = 2 * ((mine // 2 + k) % pairs) + edge
             send[j] = down_chunk(j)
 
             @pl.when(j * stride != me)

time: 23.7 us -> 23.5 us (level)
  no operation moved by 1% of the time
where the time goes in v4:
time: 23.5 us; the launch traced here: 23.3 us
  Pallas kernels  20.8 us (89%)
  local copies, waits for them, and re-layouts  1.89 us (8%)
  between operations  0.65 us (3%)
    pallas_call x1, Pallas kernels, body(): pl.pallas_call(functools.partial(kernel, tm_count, space_count), out_shap...  19.9 us
    unnamed x4, local copies, waits for them, and re-layouts  1.89 us
    pallas_call x1, Pallas kernels, body(): pl.pallas_call(spread_out, out_shape=(out, out), in_specs=[vmem], out_spe...  0.92 us

profile of v4, /device:TPU:1, one launch (start us, length us, event | category | flops | bytes accessed | tf_op | source)
XLA Modules:
  0.0 23.3 jit_solution(5658052003567520288)
XLA Ops:
  0.6 0.0 copy-start
  0.6 0.9 %copy-done = s32[8,32,256]{2,1,0:T(8,128)S(1)} copy-done((s32[8,32,256]{2,1,0:T(8,128)S(1)}, s32[8,32,256]{2,1,0:T(8,128)}, u32[]{:S(2)}) %copy-start) | copy-done | bytes 262168
  1.6 0.0 copy-start.1
  1.6 0.9 %copy-done.1 = s32[8,32,256]{2,1,0:T(8,128)S(1)} copy-done((s32[8,32,256]{2,1,0:T(8,128)S(1)}, s32[8,32,256]{2,1,0:T(8,128)}, u32[]{:S(2)}) %copy-start.1) | copy-done | bytes 262168
  2.5 19.9 %shard_map.41.landed = f32[8,2,8,8,128]{4,3,2,1,0:T(8,128)S(1)} custom-call(s32[8,32,256]{2,1,0:T(8,128)S(1)} %copy-done, s32[8,32,256]{2,1,0:T(8,128)S(1)} %copy-done.1), custom_call_target="tpu_custom_call" | custom-call | tf_op jit(solution)/shard_map/pallas_call | solution.py:336
  22.4 0.9 %shard_map.42 = (f32[8,32,256]{2,1,0:T(8,128)}, f32[8,32,256]{2,1,0:T(8,128)}) custom-call(f32[8,2,8,8,128]{4,3,2,1,0:T(8,128)S(1)} %shard_map.41.landed), custom_call_target="tpu_custom_call" | custom-call | tf_op jit(solution)/shard_map/pallas_call | solution.py:363
Async XLA Ops:
  0.6 1.0 %copy-start = (s32[8,32,256]{2,1,0:T(8,128)S(1)}, s32[8,32,256]{2,1,0:T(8,128)}, u32[]{:S(2)}) copy-start(s32[8,32,256]{2,1,0:T(8,128)} %hits_hbm.1) | copy-start | bytes 786436
  1.6 0.9 %copy-start.1 = (s32[8,32,256]{2,1,0:T(8,128)S(1)}, s32[8,32,256]{2,1,0:T(8,128)}, u32[]{:S(2)}) copy-start(s32[8,32,256]{2,1,0:T(8,128)} %misses_hbm.1) | copy-start | bytes 786436
